TPU v7x, 128 devices: a whole 4x4x4 slice. The times are simulated.
128 devices in a mesh: dp: 8 (over z, core), mp: 16 (over x, y).
Axes of the slice: x: 4, y: 4, z: 4, core: 2. Of those that a mesh axis runs over, the one named last changes fastest.
Arguments:
- activations: bfloat16 [16384, 5120], P(('dp', 'mp')), may hold values from -10 to 10
- cotangent: bfloat16 [16384, 5120], P('dp', 'mp'), may hold values from -1 to 1
- master_weights: float32 [5120, 5120], P('dp', 'mp'), may hold values from -32 to 32
- first_moment: float32 [5120, 5120], P('dp', 'mp'), may hold values from -1 to 1
- second_moment: float32 [5120, 5120], P('dp', 'mp'), may hold values from 0.25 to 4
- step_count: int32 [1], replicated, may hold values from 1 to 23
- language_ids: int32 [1], replicated, may hold values from 0 to 7
- language_rates: float32 [8], replicated, may hold values from 0.25 to 2
Outputs:
- new_master: float32 [5120, 5120], P('dp', 'mp')
- new_first: float32 [5120, 5120], P('dp', 'mp')
- new_second: float32 [5120, 5120], P('dp', 'mp')
- new_weights: bfloat16 [5120, 5120], P(None, 'mp')
All inputs are finite; a program needn't handle non-finite values.
Results may differ from a plain program's by a relative error of at most 0.0004.
Values may be sent and summed in bfloat16 or wider, within the bound.
No kernel may reach another device: no remote copies, remote signals or barrier semaphores. Data moves between devices by JAX's collectives and lax.ppermute only.
A program may use at most 128 MiB of HBM per device.

v0:
```python
import jax
import jax.numpy as jnp
from jax import lax
from jax.sharding import PartitionSpec as P

beta_one = 0.9
beta_two = 0.999
epsilon = 1e-06
decay_weight = 0.1
base_rate = 0.25


def on_device(
    activations,
    cotangent,
    master_weights,
    first_moment,
    second_moment,
    step_count,
    language_ids,
    language_rates,
):
    gathered = lax.all_gather(activations, "mp", axis=0, tiled=True)
    gradient = lax.psum_scatter(
        lax.dot_general(
            gathered, cotangent, (((0,), (0,)), ((), ())), preferred_element_type=jnp.float32
        ),
        "dp",
        scatter_dimension=0,
        tiled=True,
    )
    steps_done = step_count[0].astype(jnp.float32)
    corr_one = 1.0 - jnp.power(jnp.float32(beta_one), steps_done)
    corr_two = 1.0 - jnp.power(jnp.float32(beta_two), steps_done)
    new_first = beta_one * first_moment + (1.0 - beta_one) * gradient
    new_second = beta_two * second_moment + (1.0 - beta_two) * gradient * gradient
    update = (
        new_first / corr_one / (jnp.sqrt(new_second / corr_two) + epsilon)
        + decay_weight * master_weights
    )
    weight_sq, update_sq = lax.psum(
        (jnp.sum(master_weights * master_weights), jnp.sum(update * update)), ("dp", "mp")
    )
    trust = jnp.sqrt(weight_sq) / jnp.sqrt(update_sq)
    picked = jnp.arange(language_rates.shape[0], dtype=jnp.int32) == language_ids[0]
    rate = base_rate * jnp.sum(jnp.where(picked, language_rates, jnp.float32(0.0)))
    new_master = master_weights - rate * trust * update
    new_weights = lax.all_gather(new_master.astype(jnp.bfloat16), "dp", axis=0, tiled=True)
    return (new_master, new_first, new_second, new_weights)


def solution(mesh):
    return jax.shard_map(
        on_device,
        mesh=mesh,
        in_specs=(
            P(("dp", "mp"), None),
            P("dp", "mp"),
            P("dp", "mp"),
            P("dp", "mp"),
            P("dp", "mp"),
            P(),
            P(),
            P(),
        ),
        out_specs=(P("dp", "mp"), P("dp", "mp"), P("dp", "mp"), P(None, "mp")),
        check_vma=False,
    )
```

profile of v0, /device:TPU:1, one launch (start us, length us, event | category | flops | bytes accessed | tf_op | source)
XLA Modules:
  0.0 311.8 jit_solution(5477487466860797035)
XLA Ops:
  7.2 0.0 copy-start
  7.2 0.0 all-gather.3.cloned.1.call-start
  7.2 0.7 all-gather.3.cloned.1.call-update
  7.9 0.0 reduce-scatter.2.cloned.1.call-start
  8.0 138.1 %all-gather.3.cloned.1.call-done = bf16[2048,5120]{1,0:T(8,128)(2,1)} async-done(((bf16[128,5120]{1,0:T(8,128)(2,1)}), bf16[2048,5120]{1,0:T(8,128)(2,1)}) %all-gather.3.cloned.1.call-update) | async-done | bytes 20971536 | tf_op jit(solution)/shard_map/all_gather | solution.py:23
  146.0 0.0 copy-done
  146.0 13.9 %fusion.4 = f32[5120,320]{0,1:T(8,128)} fusion(bf16[2048,320]{0,1:T(8,128)(2,1)S(1)} %copy-done, bf16[2048,5120]{1,0:T(8,128)(2,1)} %all-gather.3.cloned.1.call-done), kind=kOutput, calls=%fused_computation.10 | convolution fusion | flops 6710886400 | bytes 28835840 | tf_op jit(solution)/shard_map/dot_general | solution.py:25
  159.9 0.0 copy-start.2
  159.9 0.0 copy-start.1
  159.9 0.0 reduce-scatter.2.cloned.1.call-update
  160.0 0.0 all-gather.5.cloned.1.call-start
  161.5 0.0 copy-done.2
  161.5 0.6 fusion.1
  162.7 40.4 %reduce-scatter.2.cloned.1.call-done = f32[640,320]{0,1:T(8,128)} async-done(((f32[5120,320]{0,1:T(8,128)}), f32[640,320]{0,1:T(8,128)}) %reduce-scatter.2.cloned.1.call-update) | async-done | bytes 819216 | tf_op jit(solution)/shard_map/reduce_scatter | solution.py:24
  203.1 0.0 copy-done.1
  203.1 4.1 %multiply_reduce_fusion = (f32[]{:T(128)}, f32[640,320]{0,1:T(8,128)S(1)}, f32[640,320]{0,1:T(8,128)}, f32[640,320]{0,1:T(8,128)}, f32[]{:T(128)}) fusion(f32[640,320]{0,1:T(8,128)S(1)} %copy-done.1, f32[]{:T(128)} %bitcast.2, f32[]{:T(128)} %bitcast.1, f32[640,320]{0,1:T(8,128)} %reduce-scatter.2.cloned.1.call-done, f32[640,320]{0,1:T(8,128)} %param.12, ...), kind=kLoop, calls=%fused_computation.3 | loop fusion | flops 3481598 | bytes 5734416 | tf_op jit(solution)/shard_map/reduce_sum | solution.py:42
  207.2 66.1 %all-reduce = (f32[]{:T(128)}, f32[]{:T(128)}) all-reduce(f32[]{:T(128)} %get-tuple-element.12, f32[]{:T(128)} %get-tuple-element.8), channel_id=1, replica_groups=mesh['dp'=8,'mp'=16] {'dp','mp'}, use_global_device_ids=true, to_apply=%region_2.0 | all-reduce | flops 2 | bytes 16 | tf_op jit(solution)/shard_map/psum | solution.py:41
  274.7 1.1 fusion.2
  275.8 0.0 all-gather.5.cloned.1.call-update
  275.8 25.6 %all-gather.5.cloned.1.call-done = bf16[5120,320]{0,1:T(8,128)(2,1)} async-done(((bf16[640,320]{0,1:T(8,128)(2,1)}), bf16[5120,320]{0,1:T(8,128)(2,1)}) %all-gather.5.cloned.1.call-update) | async-done | bytes 3276816 | tf_op jit(solution)/shard_map/all_gather | solution.py:48
  301.4 3.8 %copy.15 = bf16[5120,320]{0,1:T(8,128)(2,1)} copy(bf16[5120,320]{0,1:T(8,128)(2,1)} %all-gather.5.cloned.1.call-done) | data formatting | bytes 6553600
Async XLA Ops:
  7.2 138.9 %copy-start = (bf16[2048,320]{0,1:T(8,128)(2,1)S(1)}, bf16[2048,320]{0,1:T(8,128)(2,1)}, u32[]{:S(2)}) copy-start(bf16[2048,320]{0,1:T(8,128)(2,1)} %param.9) | copy-start | bytes 3932164
  7.2 138.9 %all-gather.3.cloned.1.call-start = ((), (), s32[]{:S(2)}) async-start(), calls=%async_computation.1 | async-start | bytes 22282240 | tf_op jit(solution)/shard_map/all_gather | solution.py:23
  7.9 195.2 %reduce-scatter.2.cloned.1.call-start = ((), (), s32[]{:S(2)}) async-start(), calls=%async_computation.2 | async-start | bytes 7372800 | tf_op jit(solution)/shard_map/reduce_scatter | solution.py:24
  159.9 1.5 copy-start.2
  159.9 43.2 %copy-start.1 = (f32[640,320]{0,1:T(8,128)S(1)}, f32[640,320]{0,1:T(8,128)}, u32[]{:S(2)}) copy-start(f32[640,320]{0,1:T(8,128)} %param.10) | copy-start | bytes 2457604
  160.0 141.4 %all-gather.5.cloned.1.call-start = ((), (), s32[]{:S(2)}) async-start(), calls=%async_computation.3 | async-start | bytes 3686400 | tf_op jit(solution)/shard_map/all_gather | solution.py:48
Sparse Core Ops, SparseCore 0:
  10.2 135.8 all-gather.2
  160.1 42.9 reduce-scatter.1
  276.0 25.3 all-gather.4
where the time goes:
time: 312 us
  waiting for transfers between devices  205 us (66%)
  blocking collectives  66.1 us (21%)
  between operations  17.2 us (6%)
  matrix products  13.9 us (4%)
  other arithmetic  5.83 us (2%)
  local copies, waits for them, and re-layouts  3.86 us (1%)
    all_gather x1, waiting for transfers between devices, on_device(): gathered = lax.all_gather(activations, 'mp', axis=0, tiled=True)  138 us
    psum x1, blocking collectives, on_device(): lax.psum((jnp.sum(master_weights * master_weights), jnp.sum(update * upda...  66.1 us
    reduce_scatter x1, waiting for transfers between devices, on_device(): lax.psum_scatter(lax.dot_general(gathered, cotangent, (((0,), (0,)), ((),...  40.4 us
    all_gather x1, waiting for transfers between devices, on_device(): lax.all_gather(new_master.astype(jnp.bfloat16), 'dp', axis=0, tiled=True)  25.6 us
    dot_general x1, matrix products, on_device(): lax.dot_general(gathered, cotangent, (((0,), (0,)), ((), ())), preferred_...  13.9 us
  transfers between devices with their start and end apart: 3, of which 3 were waited for; matrix products, arithmetic and copies ran while one was open for 0% of the time, Pallas kernels for 0%

commit v1 on v0

--- a/solution.py
+++ b/solution.py
@@ -45,7 +45,15 @@
     picked = jnp.arange(language_rates.shape[0], dtype=jnp.int32) == language_ids[0]
     rate = base_rate * jnp.sum(jnp.where(picked, language_rates, jnp.float32(0.0)))
     new_master = master_weights - rate * trust * update
-    new_weights = lax.all_gather(new_master.astype(jnp.bfloat16), "dp", axis=0, tiled=True)
+    new_weights = jnp.concatenate(
+        lax.all_to_all(
+            jnp.stack([new_master.astype(jnp.bfloat16)] * lax.axis_size("dp"), axis=0),
+            axis_name="dp",
+            split_axis=0,
+            concat_axis=0,
+        ),
+        axis=0,
+    )
     return (new_master, new_first, new_second, new_weights)
 
 

time: 312 us -> 328 us (1.051)
  blocking collectives: 66.1 us -> 109 us
  waiting for transfers between devices: 205 us -> 179 us
    all_to_all x0 -> x1, blocking collectives: none -> 42.9 us  [on_device(): lax.all_to_all(jnp.stack([new_master.astype(jnp.bfloat16)] * lax.axis_siz...]
    all_gather x1 -> x0, waiting for transfers between devices: 25.6 us -> none  [on_device(): lax.all_gather(new_master.astype(jnp.bfloat16), 'dp', axis=0, tiled=True)]
    unnamed x7 -> x6, local copies, waits for them, and re-layouts: 3.86 us -> 0.02 us
  transfers between devices with their start and end apart: 3 -> 2, of which waited for: 3 -> 2; matrix products, arithmetic and copies ran while one was open for 0% -> 0% of each run, Pallas kernels for 0% -> 0%
where the time goes in v1:
time: 328 us
  waiting for transfers between devices  179 us (55%)
  blocking collectives  109 us (33%)
  between operations  17.6 us (5%)
  matrix products  13.9 us (4%)
  other arithmetic  5.7 us (2%)
    all_gather x1, waiting for transfers between devices, on_device(): gathered = lax.all_gather(activations, 'mp', axis=0, tiled=True)  138 us
    psum x1, blocking collectives, on_device(): lax.psum((jnp.sum(master_weights * master_weights), jnp.sum(update * upda...  66.1 us
    all_to_all x1, blocking collectives, on_device(): lax.all_to_all(jnp.stack([new_master.astype(jnp.bfloat16)] * lax.axis_siz...  42.9 us
    reduce_scatter x1, waiting for transfers between devices, on_device(): lax.psum_scatter(lax.dot_general(gathered, cotangent, (((0,), (0,)), ((),...  40.4 us
    dot_general x1, matrix products, on_device(): lax.dot_general(gathered, cotangent, (((0,), (0,)), ((), ())), preferred_...  13.9 us
  transfers between devices with their start and end apart: 2, of which 2 were waited for; matrix products, arithmetic and copies ran while one was open for 0% of the time, Pallas kernels for 0%

profile of v1, /device:TPU:1, one launch (start us, length us, event | category | flops | bytes accessed | tf_op | source)
XLA Modules:
  0.0 327.9 jit_solution(2286281235317851598)
XLA Ops:
  7.2 0.0 copy-start
  7.2 0.0 all-gather.2.cloned.1.call-start
  7.2 0.7 all-gather.2.cloned.1.call-update
  7.9 0.0 reduce-scatter.2.cloned.1.call-start
  8.0 138.1 %all-gather.2.cloned.1.call-done = bf16[2048,5120]{1,0:T(8,128)(2,1)} async-done(((bf16[128,5120]{1,0:T(8,128)(2,1)}), bf16[2048,5120]{1,0:T(8,128)(2,1)}) %all-gather.2.cloned.1.call-update) | async-done | bytes 20971536 | tf_op jit(solution)/shard_map/all_gather | solution.py:23
  146.0 0.0 copy-done
  146.1 13.9 %fusion.4 = f32[5120,320]{0,1:T(8,128)} fusion(bf16[2048,320]{0,1:T(8,128)(2,1)S(1)} %copy-done, bf16[2048,5120]{1,0:T(8,128)(2,1)} %all-gather.2.cloned.1.call-done), kind=kOutput, calls=%fused_computation.10 | convolution fusion | flops 6710886400 | bytes 28835840 | tf_op jit(solution)/shard_map/dot_general | solution.py:25
  159.9 0.0 copy-start.2
  159.9 0.0 copy-start.1
  159.9 0.0 reduce-scatter.2.cloned.1.call-update
  161.4 0.0 copy-done.2
  161.4 0.6 fusion.1
  162.7 40.4 %reduce-scatter.2.cloned.1.call-done = f32[640,320]{0,1:T(8,128)} async-done(((f32[5120,320]{0,1:T(8,128)}), f32[640,320]{0,1:T(8,128)}) %reduce-scatter.2.cloned.1.call-update) | async-done | bytes 819216 | tf_op jit(solution)/shard_map/reduce_scatter | solution.py:24
  203.1 0.0 copy-done.1
  203.1 4.1 %multiply_reduce_fusion = (f32[]{:T(128)}, f32[640,320]{0,1:T(8,128)S(1)}, f32[640,320]{0,1:T(8,128)}, f32[640,320]{0,1:T(8,128)}, f32[]{:T(128)}) fusion(f32[640,320]{0,1:T(8,128)S(1)} %copy-done.1, f32[]{:T(128)} %bitcast.2, f32[]{:T(128)} %bitcast.1, f32[640,320]{0,1:T(8,128)} %reduce-scatter.2.cloned.1.call-done, f32[640,320]{0,1:T(8,128)} %param.12, ...), kind=kLoop, calls=%fused_computation.3 | loop fusion | flops 3481598 | bytes 5734416 | tf_op jit(solution)/shard_map/reduce_sum | solution.py:42
  207.2 66.1 %all-reduce = (f32[]{:T(128)}, f32[]{:T(128)}) all-reduce(f32[]{:T(128)} %get-tuple-element.12, f32[]{:T(128)} %get-tuple-element.8), channel_id=1, replica_groups=mesh['dp'=8,'mp'=16] {'dp','mp'}, use_global_device_ids=true, to_apply=%region_2.0 | all-reduce | flops 2 | bytes 16 | tf_op jit(solution)/shard_map/psum | solution.py:41
  274.7 1.0 fusion.2
  275.7 0.3 stack.2
  275.9 42.9 %all_to_all.5 = bf16[8,640,320]{1,2,0:T(8,128)(2,1)S(1)} all-to-all(bf16[8,640,320]{1,2,0:T(8,128)(2,1)S(1)} %stack.2), channel_id=1, replica_groups=mesh['dp'=8,'mp'=16] {'dp'}, dimensions={0} | all-to-all | bytes 6553600 | tf_op jit(solution)/shard_map/all_to_all | solution.py:49
  318.8 2.2 copy.13
Async XLA Ops:
  7.2 138.9 %copy-start = (bf16[2048,320]{0,1:T(8,128)(2,1)S(1)}, bf16[2048,320]{0,1:T(8,128)(2,1)}, u32[]{:S(2)}) copy-start(bf16[2048,320]{0,1:T(8,128)(2,1)} %param.9) | copy-start | bytes 3932164
  7.2 138.9 %all-gather.2.cloned.1.call-start = ((), (), s32[]{:S(2)}) async-start(), calls=%async_computation.2 | async-start | bytes 22282240 | tf_op jit(solution)/shard_map/all_gather | solution.py:23
  7.9 195.2 %reduce-scatter.2.cloned.1.call-start = ((), (), s32[]{:S(2)}) async-start(), calls=%async_computation.3 | async-start | bytes 7372800 | tf_op jit(solution)/shard_map/reduce_scatter | solution.py:24
  159.9 1.5 copy-start.2
  159.9 43.2 %copy-start.1 = (f32[640,320]{0,1:T(8,128)S(1)}, f32[640,320]{0,1:T(8,128)}, u32[]{:S(2)}) copy-start(f32[640,320]{0,1:T(8,128)} %param.10) | copy-start | bytes 2457604
Sparse Core Ops, SparseCore 0:
  10.2 135.7 all-gather.1
  160.1 42.9 reduce-scatter.1
